TPU v7x, 512 devices: a whole 4x8x8 slice. The times are simulated.
512 devices in a mesh: row: 32 (over z, x), col: 16 (over y, core).
Axes of the slice: x: 4, y: 8, z: 8, core: 2. Of those that a mesh axis runs over, the one named last changes fastest.
Arguments:
- rhs: bfloat16 [524288, 256], P(('row', 'col')), may hold values from -6 to 6
- order: int32 [512, 1024], P(('row', 'col')), may hold values from 0 to 1023, each once within a row
- leaf_inverse: bfloat16 [1024, 512, 512], P(('row', 'col')), may hold values from -1 to 2
- leaf_column_generator: bfloat16 [1024, 512, 256], P(('row', 'col')), may hold values from -0.25 to 0.25
- factor_up: bfloat16 [512, 9, 256, 256], P(('row', 'col')), may hold values from -1 to 1
- downward_coupling_factors: bfloat16 [512, 9, 256, 256], P(('row', 'col')), may hold values from -1 to 2
Outputs:
- solution: bfloat16 [524288, 256], P(('row', 'col'))
All inputs are finite; a program needn't handle non-finite values.
Results may differ from a plain program's by a relative error of at most 0.015.
Values may be sent and summed in bfloat16 or wider, within the bound.
No kernel may reach another device: no remote copies, remote signals or barrier semaphores. Data moves between devices by JAX's collectives and lax.ppermute only.
A program may use at most 64 MiB of HBM per device.

v0:
```python
import functools

import functools

import jax
import jax.numpy as jnp
from jax import lax
from jax.experimental import pallas as pl
from jax.experimental.pallas import tpu as pltpu
from jax.sharding import PartitionSpec as P


BF16 = jnp.bfloat16
F32 = jnp.float32
MIB = 1 << 20


def pair_groups(size, bit):
    step = 1 << bit
    return [[i, i ^ step] for i in range(size) if not i & step]


def axis_of(level, col_bits):
    return ("col", level) if level < col_bits else ("row", level - col_bits)


def both(value, level, col_bits):
    axis, bit = axis_of(level, col_bits)
    groups = pair_groups(lax.axis_size(axis), bit)
    return lax.all_gather(value, axis, axis=0, tiled=False, axis_index_groups=groups)


def across_both(value, level, col_bits):
    axis, bit = axis_of(level, col_bits)
    step, size = 1 << bit, lax.axis_size(axis)
    groups = [[i, i ^ (3 * step)] for i in range(size) if not i & (2 * step)]
    return lax.all_gather(value, axis, axis=0, tiled=False, axis_index_groups=groups)


def among_four(value, level, col_bits):
    axis, bit = axis_of(level, col_bits)
    step, size = 1 << bit, lax.axis_size(axis)
    groups = [[i + step * k for k in range(4)] for i in range(size) if not i & (3 * step)]
    return lax.all_to_all(value, axis, 0, 0, axis_index_groups=groups)


def group_index(level, col_bits):
    axis, bit = axis_of(level, col_bits)
    return lax.rem(lax.div(lax.axis_index(axis), 1 << bit), 4)


def toggle(index, step):
    return step - 2 * step * lax.rem(lax.div(index, step), 2)


def partner_slot(level, col_bits):
    axis, bit = axis_of(level, col_bits)
    return 1 - lax.rem(lax.div(lax.axis_index(axis), 1 << bit), 2)


def times(a, b):
    return jnp.dot(a, b, preferred_element_type=F32)


def times_transposed(a, b):
    return lax.dot_general(a, b, (((0,), (0,)), ((), ())), preferred_element_type=F32)


def pair_sum(pair_ref):
    return pair_ref[0].astype(F32) + pair_ref[1].astype(F32)


def call(kernel, outs, n_in, limit):
    vmem = [pl.BlockSpec(memory_space=pltpu.VMEM)] * n_in
    return pl.pallas_call(
        kernel,
        out_shape=[jax.ShapeDtypeStruct(shape, dtype) for shape, dtype in outs],
        in_specs=vmem,
        out_specs=[pl.BlockSpec(memory_space=pltpu.VMEM)] * len(outs),
        compiler_params=pltpu.CompilerParams(vmem_limit_bytes=limit),
    )


def leaf_kernel(
    low, col_bits, order_hbm, rhs_hbm, inverse_hbm, basis_hbm, up_hbm, down_hbm, rows_hbm, state_hbm, term_ref, share_hbm,
    order_ref, rhs_ref, inverse_ref, basis_ref, up_ref, share_ref, rows_ref, state_ref, sems, share_sems, out_sems,
):
    last = up_hbm.shape[1] - 1
    me = group_index(low, col_bits)
    rows = rhs_ref.shape[0]
    leaves, leaf = inverse_ref.shape[:2]
    moves = [
        pltpu.make_async_copy(src, dst, sems.at[k])
        for k, (src, dst) in enumerate(
            [
                (order_hbm, order_ref),
                (rhs_hbm, rhs_ref),
                (inverse_hbm, inverse_ref),
                (basis_hbm, basis_ref),
                (up_hbm.at[0, 0], up_ref),
                (down_hbm.at[0, last - 1], share_ref.at[0]),
                (up_hbm.at[0, last], share_ref.at[1]),
                (down_hbm.at[0, last], share_ref.at[2]),
            ]
        )
    ]
    for move in moves:
        move.start()
    moves[0].wait()
    across = jnp.broadcast_to(order_ref[...], (128, rows)).T.astype(jnp.int16)
    lane = lax.broadcasted_iota(jnp.int16, (rows, 128), 1)
    pick = jnp.concatenate(
        [jnp.where(across == lane + jnp.int16(128 * b), BF16(1), BF16(0)) for b in range(rows // 128)],
        axis=1,
    )
    moves[1].wait()
    ordered = times(pick, rhs_ref[...]).astype(BF16)
    moves[2].wait()
    moves[3].wait()
    for move in moves[5:]:
        move.wait()
    near, across_pair = me + toggle(me, 1), me + toggle(me, 2)
    slots = [(near, 0), (across_pair, 1), (near + across_pair - me, 1), (me, 1)]
    spread = [
        pltpu.make_async_copy(share_ref.at[first : first + 2], share_hbm.at[slot], share_sems.at[k])
        for k, (slot, first) in enumerate(slots)
    ]
    for move in spread:
        move.start()
    state, keep = None, []
    for j in range(leaves):
        block = times(inverse_ref[j], ordered[j * leaf : (j + 1) * leaf])
        rows_ref[j] = block
        keep.append(pltpu.make_async_copy(rows_ref.at[j], rows_hbm.at[j], out_sems.at[j]))
        keep[-1].start()
        part = times_transposed(basis_ref[j], block.astype(BF16))
        state = part if state is None else state + part
    state_ref[...] = state
    keep.append(pltpu.make_async_copy(state_ref, state_hbm, out_sems.at[leaves]))
    keep[-1].start()
    moves[4].wait()
    term_ref[...] = times(up_ref[...], state.astype(BF16)).astype(BF16)
    for move in spread + keep:
        move.wait()


def up_kernel(level, pair_ref, up_ref, term_ref):
    term_ref[...] = times(up_ref[0, level], pair_sum(pair_ref).astype(BF16)).astype(BF16)


def state_kernel(pair_ref, half_ref):
    half_ref[...] = pair_sum(pair_ref).astype(BF16)


def top_kernel(low, col_bits, terms_ref, half_ref, share_ref, saved_ref, up_ref, down_ref, y_ref, sent_ref):
    me = group_index(low, col_bits)
    flip, across = toggle(me, 1), toggle(me, 2)
    b, c, d = me + flip, me + across, me + flip + across

    def rounded(x):
        return x.astype(BF16)

    def elim(factor, value):
        return rounded(times(factor, value)).astype(F32)

    def above(factor, coupling, state, value):
        coupled = rounded(times(coupling, value)).astype(F32)
        return rounded(state + 0.5 * (coupled - times_transposed(factor, value)))

    mine, near = up_ref[0, low + 1], share_ref[b, 1]
    state = pair_sum(terms_ref)
    other = 1 - lax.div(me, 2)
    state_half, far_half = half_ref[1 - other], half_ref[other]
    y_mine = rounded(elim(mine, state_half) + elim(share_ref[c, 0], far_half))
    y_near = rounded(elim(near, state_half) + elim(share_ref[d, 0], far_half))
    top_mine = above(mine, share_ref[c, 1], state, y_mine)
    top_near = above(near, share_ref[d, 1], state, y_near)
    coupled = rounded(times(share_ref[b, 0], top_near)).astype(F32)
    top = rounded(pair_sum(saved_ref) + 0.5 * (coupled - times_transposed(up_ref[0, low], top_mine)))
    y_ref[...] = top
    sent_ref[...] = rounded(times(down_ref[0, low - 1], top))


def down_kernel(level, col_bits, pair_ref, saved_ref, above_ref, up_ref, down_ref, y_ref, sent_ref):
    coupled = pair_ref[partner_slot(level, col_bits)].astype(F32)
    top = pair_sum(saved_ref) + 0.5 * (coupled - times_transposed(up_ref[0, level], above_ref[...]))
    y_ref[...] = top.astype(BF16)
    sent_ref[...] = times(down_ref[0, level - 1], top.astype(BF16)).astype(BF16)


def last_kernel(
    col_bits, order_ref, pair_ref, state_ref, above_ref, up_ref, inverse_ref, basis_ref, rows_ref, out_ref
):
    rows = out_ref.shape[0]
    leaves = inverse_ref.shape[0]
    coupled = pair_ref[partner_slot(0, col_bits)].astype(F32)
    top = state_ref[...] + 0.5 * (coupled - times_transposed(up_ref[0, 0], above_ref[...]))
    top_half = top.astype(BF16)
    solved = []
    for j in range(leaves):
        back = times(basis_ref[j], top_half).astype(BF16)
        solved.append((rows_ref[j] - times(inverse_ref[j], back)).astype(BF16))
    place = lax.broadcasted_iota(jnp.int16, (rows, rows), 0) == order_ref[...].astype(jnp.int16)
    pick = jnp.where(place, BF16(1), BF16(0))
    out_ref[...] = times(pick, jnp.concatenate(solved, axis=0)).astype(BF16)


def on_device(
    rhs, order, leaf_inverse, leaf_column_generator, factor_up, downward_coupling_factors
):
    leaves, leaf = leaf_inverse.shape[:2]
    rank = leaf_column_generator.shape[2]
    genes = rhs.shape[1]
    levels = factor_up.shape[1]
    last = levels - 1
    low = last - 1
    col_bits = lax.axis_size("col").bit_length() - 1
    up, down = factor_up, downward_coupling_factors
    small = (rank, genes)
    steps = [(small, BF16), (small, BF16)]

    rows, state, term, share = pl.pallas_call(
        functools.partial(leaf_kernel, low, col_bits),
        out_shape=[
            jax.ShapeDtypeStruct((leaves, leaf, genes), F32),
            jax.ShapeDtypeStruct(small, F32),
            jax.ShapeDtypeStruct(small, BF16),
            jax.ShapeDtypeStruct((4, 2) + factor_up.shape[2:], BF16),
        ],
        in_specs=[pl.BlockSpec(memory_space=pltpu.HBM)] * 6,
        out_specs=[pl.BlockSpec(memory_space=pltpu.VMEM if k == 2 else pltpu.HBM) for k in range(4)],
        scratch_shapes=[
            pltpu.VMEM(order.shape, order.dtype),
            pltpu.VMEM(rhs.shape, BF16),
            pltpu.VMEM(leaf_inverse.shape, BF16),
            pltpu.VMEM(leaf_column_generator.shape, BF16),
            pltpu.VMEM(factor_up.shape[2:], BF16),
            pltpu.VMEM((3,) + factor_up.shape[2:], BF16),
            pltpu.VMEM((leaves, leaf, genes), F32),
            pltpu.VMEM(small, F32),
            pltpu.SemaphoreType.DMA((8,)),
            pltpu.SemaphoreType.DMA((4,)),
            pltpu.SemaphoreType.DMA((leaves + 1,)),
        ],
        compiler_params=pltpu.CompilerParams(vmem_limit_bytes=56 * MIB),
    )(order, rhs, leaf_inverse, leaf_column_generator, up, down)
    pairs = [both(term, 0, col_bits)]
    shared = among_four(share, low, col_bits)
    for level in range(1, low):
        (term,) = call(functools.partial(up_kernel, level), [(small, BF16)], 2, 4 * MIB)(pairs[-1], up)
        pairs.append(both(term, level, col_bits))
    (term,) = call(functools.partial(up_kernel, low), [(small, BF16)], 2, 4 * MIB)(pairs[-1], up)
    term, shared = lax.optimization_barrier((term, shared))
    terms = both(term, low, col_bits)
    (half,) = call(state_kernel, [(small, BF16)], 1, 4 * MIB)(terms)
    y, sent = call(functools.partial(top_kernel, low, col_bits), steps, 6, 8 * MIB)(
        terms, across_both(half, low, col_bits), shared, pairs[-1], up, down
    )
    for level in range(low - 1, 0, -1):
        y, sent = call(functools.partial(down_kernel, level, col_bits), steps, 5, 6 * MIB)(
            both(sent, level, col_bits), pairs[level - 1], y, up, down
        )
    (solved,) = call(functools.partial(last_kernel, col_bits), [(rhs.shape, BF16)], 8, 24 * MIB)(
        order, both(sent, 0, col_bits), state, y, up, leaf_inverse, leaf_column_generator, rows
    )
    return solved


def solution(mesh):
    in_specs = (
        P(("row", "col"), None),
        P(("row", "col"), None),
        P(("row", "col"), None, None),
        P(("row", "col"), None, None),
        P(("row", "col"), None, None, None),
        P(("row", "col"), None, None, None),
    )
    out_specs = P(("row", "col"), None)

    return jax.shard_map(on_device, mesh=mesh, in_specs=in_specs, out_specs=out_specs, check_vma=False)
```

profile of v0, /device:TPU:1, one launch (start us, length us, event | category | flops | bytes accessed | tf_op | source)
XLA Modules:
  0.0 134.7 jit_solution(16621933765938001275)
XLA Ops:
  0.0 4.7 %shard_map.64 = (f32[2,512,256]{2,1,0:T(8,128)}, f32[256,256]{1,0:T(8,128)}, bf16[256,256]{1,0:T(8,128)(2,1)}, bf16[4,2,256,256]{3,2,1,0:T(8,128)(2,1)}) custom-call(s32[1,1024]{1,0:T(1,128)} %order_ref.1, bf16[1024,256]{1,0:T(8,128)(2,1)} %rhs_hbm.1, bf16[2,512,512]{2,1,0:T(8,128)(2,1)} %inverse_ref.1, bf16[2,512,256]{2,1,0:T(8,128)(2,1)} %basis_ref.1, ...), custom_call_target="tpu_custom_call" | custom-call | tf_op jit(solution)/shard_map/pallas_call | solution.py:222
  4.7 11.0 %all-to-all-start = ((bf16[4,2,256,256]{3,2,1,0:T(8,128)(2,1)}), bf16[4,2,256,256]{3,2,1,0:T(8,128)(2,1)S(1)}, u32[]{:S(2)}, u32[]{:S(2)}) async-start(bf16[4,2,256,256]{3,2,1,0:T(8,128)(2,1)} %get-tuple-element.26), calls=%async_computation | async-start | bytes 2097152 | tf_op jit(solution)/shard_map/all_to_all | solution.py:44
  15.7 2.6 %all-gather = bf16[512,256]{1,0:T(8,128)(2,1)S(1)} all-gather(bf16[256,256]{1,0:T(8,128)(2,1)S(1)} %copy-done.21), channel_id=2, replica_groups={{0,1},{2,3},{4,5},{6,7},{8,9},{10,11},{12,13},{14,15},{16,17},{18,19},{..., dimensions={0}, use_global_device_ids=true | all-gather | bytes 393216 | tf_op jit(solution)/shard_map/all_gather | solution.py:30
  18.5 5.3 %all-gather.1 = bf16[512,256]{1,0:T(8,128)(2,1)S(1)} all-gather(bf16[256,256]{1,0:T(8,128)(2,1)S(1)} %shard_map.65), channel_id=3, replica_groups={{0,2},{1,3},{4,6},{5,7},{8,10},{9,11},{12,14},{13,15},{16,18},{17,19},{..., dimensions={0}, use_global_device_ids=true | all-gather | bytes 393216 | tf_op jit(solution)/shard_map/all_gather | solution.py:30
  24.0 8.8 %all-gather.2 = bf16[512,256]{1,0:T(8,128)(2,1)S(1)} all-gather(bf16[256,256]{1,0:T(8,128)(2,1)S(1)} %shard_map.66), channel_id=4, replica_groups={{0,4},{1,5},{2,6},{3,7},{8,12},{9,13},{10,14},{11,15},{16,20},{17,21},{..., dimensions={0}, use_global_device_ids=true | all-gather | bytes 393216 | tf_op jit(solution)/shard_map/all_gather | solution.py:30
  33.0 10.1 %all-gather.3 = bf16[512,256]{1,0:T(8,128)(2,1)S(1)} all-gather(bf16[256,256]{1,0:T(8,128)(2,1)S(1)} %shard_map.67), channel_id=5, replica_groups={{0,8},{1,9},{2,10},{3,11},{4,12},{5,13},{6,14},{7,15},{16,24},{17,25},{..., dimensions={0}, use_global_device_ids=true | all-gather | bytes 393216 | tf_op jit(solution)/shard_map/all_gather | solution.py:30
  43.3 4.5 %all-gather.4 = bf16[512,256]{1,0:T(8,128)(2,1)S(1)} all-gather(bf16[256,256]{1,0:T(8,128)(2,1)S(1)} %shard_map.68), channel_id=6, replica_groups={{0,16},{32,48},{64,80},{96,112},{128,144},{160,176},{192,208},{224,240}..., dimensions={0}, use_global_device_ids=true | all-gather | bytes 393216 | tf_op jit(solution)/shard_map/all_gather | solution.py:30
  48.0 6.7 %all-gather.5 = bf16[512,256]{1,0:T(8,128)(2,1)S(1)} all-gather(bf16[256,256]{1,0:T(8,128)(2,1)S(1)} %shard_map.69), channel_id=7, replica_groups={{0,32},{16,48},{64,96},{80,112},{128,160},{144,176},{192,224},{208,240}..., dimensions={0}, use_global_device_ids=true | all-gather | bytes 393216 | tf_op jit(solution)/shard_map/all_gather | solution.py:30
  54.9 4.8 %all-gather.6 = bf16[512,256]{1,0:T(8,128)(2,1)S(1)} all-gather(bf16[256,256]{1,0:T(8,128)(2,1)S(1)} %shard_map.70), channel_id=8, replica_groups={{0,64},{16,80},{32,96},{48,112},{128,192},{144,208},{160,224},{176,240}..., dimensions={0}, use_global_device_ids=true | all-gather | bytes 393216 | tf_op jit(solution)/shard_map/all_gather | solution.py:30
  59.9 0.7 copy-done.15
  60.6 7.2 %all-gather.7 = bf16[512,256]{1,0:T(8,128)(2,1)S(1)} all-gather(bf16[256,256]{1,0:T(8,128)(2,1)S(1)} %shard_map.71), channel_id=9, replica_groups={{0,128},{16,144},{32,160},{48,176},{64,192},{80,208},{96,224},{112,240}..., dimensions={0}, use_global_device_ids=true | all-gather | bytes 393216 | tf_op jit(solution)/shard_map/all_gather | solution.py:30
  67.8 6.7 %all-gather.8 = bf16[512,256]{1,0:T(8,128)(2,1)S(1)} all-gather(bf16[256,256]{1,0:T(8,128)(2,1)S(1)} %shard_map.72), channel_id=10, replica_groups={{0,384},{16,400},{32,416},{48,432},{64,448},{80,464},{96,480},{112,496}..., dimensions={0}, use_global_device_ids=true | all-gather | bytes 393216 | tf_op jit(solution)/shard_map/all_gather | solution.py:37
  74.5 0.9 shard_map.73
  75.5 5.8 %all-gather.9 = bf16[512,256]{1,0:T(8,128)(2,1)S(1)} all-gather(bf16[256,256]{1,0:T(8,128)(2,1)S(1)} %get-tuple-element.29), channel_id=11, replica_groups={{0,64},{16,80},{32,96},{48,112},{128,192},{144,208},{160,224},{176,240}..., dimensions={0}, use_global_device_ids=true | all-gather | bytes 393216 | tf_op jit(solution)/shard_map/all_gather | solution.py:30
  81.7 6.0 %all-gather.10 = bf16[512,256]{1,0:T(8,128)(2,1)S(1)} all-gather(bf16[256,256]{1,0:T(8,128)(2,1)S(1)} %get-tuple-element.31), channel_id=12, replica_groups={{0,32},{16,48},{64,96},{80,112},{128,160},{144,176},{192,224},{208,240}..., dimensions={0}, use_global_device_ids=true | all-gather | bytes 393216 | tf_op jit(solution)/shard_map/all_gather | solution.py:30
  87.7 0.4 shard_map.75
  88.1 4.8 %all-gather.11 = bf16[512,256]{1,0:T(8,128)(2,1)S(1)} all-gather(bf16[256,256]{1,0:T(8,128)(2,1)S(1)} %get-tuple-element.33), channel_id=13, replica_groups={{0,16},{32,48},{64,80},{96,112},{128,144},{160,176},{192,208},{224,240}..., dimensions={0}, use_global_device_ids=true | all-gather | bytes 393216 | tf_op jit(solution)/shard_map/all_gather | solution.py:30
  93.4 9.8 %all-gather.12 = bf16[512,256]{1,0:T(8,128)(2,1)S(1)} all-gather(bf16[256,256]{1,0:T(8,128)(2,1)S(1)} %get-tuple-element.35), channel_id=14, replica_groups={{0,8},{1,9},{2,10},{3,11},{4,12},{5,13},{6,14},{7,15},{16,24},{17,25},{..., dimensions={0}, use_global_device_ids=true | all-gather | bytes 393216 | tf_op jit(solution)/shard_map/all_gather | solution.py:30
  103.2 0.4 shard_map.77
  103.6 5.5 %all-gather.13 = bf16[512,256]{1,0:T(8,128)(2,1)S(1)} all-gather(bf16[256,256]{1,0:T(8,128)(2,1)S(1)} %get-tuple-element.37), channel_id=15, replica_groups={{0,4},{1,5},{2,6},{3,7},{8,12},{9,13},{10,14},{11,15},{16,20},{17,21},{..., dimensions={0}, use_global_device_ids=true | all-gather | bytes 393216 | tf_op jit(solution)/shard_map/all_gather | solution.py:30
  109.5 7.5 %all-gather.14 = bf16[512,256]{1,0:T(8,128)(2,1)S(1)} all-gather(bf16[256,256]{1,0:T(8,128)(2,1)S(1)} %get-tuple-element.39), channel_id=16, replica_groups={{0,2},{1,3},{4,6},{5,7},{8,10},{9,11},{12,14},{13,15},{16,18},{17,19},{..., dimensions={0}, use_global_device_ids=true | all-gather | bytes 393216 | tf_op jit(solution)/shard_map/all_gather | solution.py:30
  117.1 0.4 shard_map.79
  117.5 14.8 %all-gather.15 = bf16[512,256]{1,0:T(8,128)(2,1)S(1)} all-gather(bf16[256,256]{1,0:T(8,128)(2,1)S(1)} %get-tuple-element.41), channel_id=17, replica_groups={{0,1},{2,3},{4,5},{6,7},{8,9},{10,11},{12,13},{14,15},{16,17},{18,19},{..., dimensions={0}, use_global_device_ids=true | all-gather | bytes 393216 | tf_op jit(solution)/shard_map/all_gather | solution.py:30
  132.3 2.4 %shard_map.80 = bf16[1024,256]{1,0:T(8,128)(2,1)} custom-call(s32[1,1024]{1,0:T(1,128)S(1)} %copy-done.20, bf16[2,256,256]{2,1,0:T(8,128)(2,1)S(1)} %bitcast.39, f32[256,256]{1,0:T(8,128)S(1)} %copy-done.19, bf16[256,256]{1,0:T(8,128)(2,1)S(1)} %get-tuple-element.43.above_ref, bf16[1,9,256,256]{3,2,1,0:T(8,128)(2,1)S(1)} %copy-done, ...), custom_call_target="tpu_custom_call" | custom-call | tf_op jit(solution)/shard_map/pallas_call | solution.py:263
  (55 shorter events, 2.7 us)
Async XLA Ops:
  4.7 11.0 %copy-start.21 = (bf16[256,256]{1,0:T(8,128)(2,1)S(1)}, bf16[256,256]{1,0:T(8,128)(2,1)}, u32[]{:S(2)}) copy-start(bf16[256,256]{1,0:T(8,128)(2,1)} %get-tuple-element.25) | copy-start | bytes 393220
  4.7 13.6 %copy-start = (bf16[1,9,256,256]{3,2,1,0:T(8,128)(2,1)S(1)}, bf16[1,9,256,256]{3,2,1,0:T(8,128)(2,1)}, u32[]{:S(2)}) copy-start(bf16[1,9,256,256]{3,2,1,0:T(8,128)(2,1)} %up_ref.29) | copy-start | bytes 3538948
  4.7 55.9 %all-to-all-start = ((bf16[4,2,256,256]{3,2,1,0:T(8,128)(2,1)}), bf16[4,2,256,256]{3,2,1,0:T(8,128)(2,1)S(1)}, u32[]{:S(2)}, u32[]{:S(2)}) async-start(bf16[4,2,256,256]{3,2,1,0:T(8,128)(2,1)} %get-tuple-element.26), calls=%async_computation | async-start | bytes 2097152 | tf_op jit(solution)/shard_map/all_to_all | solution.py:44
  18.3 5.7 %copy-start.3 = (bf16[512,256]{1,0:T(8,128)(2,1)}, bf16[512,256]{1,0:T(8,128)(2,1)S(1)}, u32[]{:S(2)}) copy-start(bf16[512,256]{1,0:T(8,128)(2,1)S(1)} %all-gather) | copy-start | bytes 786436
  23.8 9.2 %copy-start.5 = (bf16[512,256]{1,0:T(8,128)(2,1)}, bf16[512,256]{1,0:T(8,128)(2,1)S(1)}, u32[]{:S(2)}) copy-start(bf16[512,256]{1,0:T(8,128)(2,1)S(1)} %all-gather.1) | copy-start | bytes 786436
  32.8 10.5 %copy-start.7 = (bf16[512,256]{1,0:T(8,128)(2,1)}, bf16[512,256]{1,0:T(8,128)(2,1)S(1)}, u32[]{:S(2)}) copy-start(bf16[512,256]{1,0:T(8,128)(2,1)S(1)} %all-gather.2) | copy-start | bytes 786436
  43.1 4.9 %copy-start.9 = (bf16[512,256]{1,0:T(8,128)(2,1)}, bf16[512,256]{1,0:T(8,128)(2,1)S(1)}, u32[]{:S(2)}) copy-start(bf16[512,256]{1,0:T(8,128)(2,1)S(1)} %all-gather.3) | copy-start | bytes 786436
  47.8 7.1 %copy-start.11 = (bf16[512,256]{1,0:T(8,128)(2,1)}, bf16[512,256]{1,0:T(8,128)(2,1)S(1)}, u32[]{:S(2)}) copy-start(bf16[512,256]{1,0:T(8,128)(2,1)S(1)} %all-gather.4) | copy-start | bytes 786436
  54.7 5.0 %copy-start.13 = (bf16[512,256]{1,0:T(8,128)(2,1)}, bf16[512,256]{1,0:T(8,128)(2,1)S(1)}, u32[]{:S(2)}) copy-start(bf16[512,256]{1,0:T(8,128)(2,1)S(1)} %all-gather.5) | copy-start | bytes 786436
  59.7 14.8 %copy-start.1 = (bf16[1,9,256,256]{3,2,1,0:T(8,128)(2,1)S(1)}, bf16[1,9,256,256]{3,2,1,0:T(8,128)(2,1)}, u32[]{:S(2)}) copy-start(bf16[1,9,256,256]{3,2,1,0:T(8,128)(2,1)} %down_ref.13) | copy-start | bytes 3538948
  59.9 0.7 copy-start.15
  60.6 13.9 %copy-start.16 = (bf16[512,256]{1,0:T(8,128)(2,1)S(1)}, bf16[512,256]{1,0:T(8,128)(2,1)}, u32[]{:S(2)}) copy-start(bf16[512,256]{1,0:T(8,128)(2,1)} %copy-done.15) | copy-start | bytes 786436
  74.5 6.7 %copy-start.14 = (bf16[512,256]{1,0:T(8,128)(2,1)S(1)}, bf16[512,256]{1,0:T(8,128)(2,1)}, u32[]{:S(2)}) copy-start(bf16[512,256]{1,0:T(8,128)(2,1)} %copy-done.13) | copy-start | bytes 786436
  81.3 6.4 %copy-start.12 = (bf16[512,256]{1,0:T(8,128)(2,1)S(1)}, bf16[512,256]{1,0:T(8,128)(2,1)}, u32[]{:S(2)}) copy-start(bf16[512,256]{1,0:T(8,128)(2,1)} %copy-done.11) | copy-start | bytes 786436
  87.7 5.3 %copy-start.10 = (bf16[512,256]{1,0:T(8,128)(2,1)S(1)}, bf16[512,256]{1,0:T(8,128)(2,1)}, u32[]{:S(2)}) copy-start(bf16[512,256]{1,0:T(8,128)(2,1)} %copy-done.9) | copy-start | bytes 786436
  93.0 10.2 %copy-start.8 = (bf16[512,256]{1,0:T(8,128)(2,1)S(1)}, bf16[512,256]{1,0:T(8,128)(2,1)}, u32[]{:S(2)}) copy-start(bf16[512,256]{1,0:T(8,128)(2,1)} %copy-done.7) | copy-start | bytes 786436
  103.2 5.9 %copy-start.6 = (bf16[512,256]{1,0:T(8,128)(2,1)S(1)}, bf16[512,256]{1,0:T(8,128)(2,1)}, u32[]{:S(2)}) copy-start(bf16[512,256]{1,0:T(8,128)(2,1)} %copy-done.5) | copy-start | bytes 786436
  109.1 7.9 %copy-start.4 = (bf16[512,256]{1,0:T(8,128)(2,1)S(1)}, bf16[512,256]{1,0:T(8,128)(2,1)}, u32[]{:S(2)}) copy-start(bf16[512,256]{1,0:T(8,128)(2,1)} %copy-done.3) | copy-start | bytes 786436
  117.0 15.2 %copy-start.2 = (bf16[2,512,512]{2,1,0:T(8,128)(2,1)S(1)}, bf16[2,512,512]{2,1,0:T(8,128)(2,1)}, u32[]{:S(2)}) copy-start(bf16[2,512,512]{2,1,0:T(8,128)(2,1)} %inverse_ref.1) | copy-start | bytes 3145732
  117.0 15.2 %copy-start.17 = (bf16[2,512,256]{2,1,0:T(8,128)(2,1)S(1)}, bf16[2,512,256]{2,1,0:T(8,128)(2,1)}, u32[]{:S(2)}) copy-start(bf16[2,512,256]{2,1,0:T(8,128)(2,1)} %basis_ref.1) | copy-start | bytes 1572868
  117.0 15.2 %copy-start.18 = (f32[2,512,256]{2,1,0:T(8,128)S(1)}, f32[2,512,256]{2,1,0:T(8,128)}, u32[]{:S(2)}) copy-start(f32[2,512,256]{2,1,0:T(8,128)} %get-tuple-element.44.rows_ref) | copy-start | bytes 3145732
  117.0 15.2 %copy-start.19 = (f32[256,256]{1,0:T(8,128)S(1)}, f32[256,256]{1,0:T(8,128)}, u32[]{:S(2)}) copy-start(f32[256,256]{1,0:T(8,128)} %get-tuple-element.42.state_ref) | copy-start | bytes 786436
  117.1 15.2 %copy-start.20 = (s32[1,1024]{1,0:T(1,128)S(1)}, s32[1,1024]{1,0:T(1,128)}, u32[]{:S(2)}) copy-start(s32[1,1024]{1,0:T(1,128)} %order_ref.1) | copy-start | bytes 12292
where the time goes:
time: 135 us
  blocking collectives  111 us (82%)
  Pallas kernels  11.9 us (9%)
  starting transfers between devices  11 us (8%)
    all_gather x15, blocking collectives, both(): lax.all_gather(value, axis, axis=0, tiled=False, axis_index_groups=groups)  104 us
    all_to_all x1, starting transfers between devices, among_four(): return lax.all_to_all(value, axis, 0, 0, axis_index_groups=groups)  11 us
    all_gather x1, blocking collectives, across_both(): lax.all_gather(value, axis, axis=0, tiled=False, axis_index_groups=groups)  6.69 us
    pallas_call x1, Pallas kernels, on_device(): pl.pallas_call(functools.partial(leaf_kernel, low, col_bits), out_shape=[...  4.71 us
  transfers between devices with their start and end apart: 1, of which 0 were waited for; matrix products, arithmetic and copies ran while one was open for 0% of the time, Pallas kernels for 1%

commit v1 on v0

--- a/solution.py
+++ b/solution.py
@@ -189,7 +189,7 @@
 
 
 def last_kernel(
-    col_bits, order_ref, pair_ref, state_ref, above_ref, up_ref, inverse_ref, basis_ref, rows_ref, out_ref
+    col_bits, order_ref, pair_ref, state_ref, above_ref, up_ref, inverse_ref, basis_ref, rows_ref, out_hbm, out_ref, sems
 ):
     rows = out_ref.shape[0]
     leaves = inverse_ref.shape[0]
@@ -202,7 +202,16 @@
         solved.append((rows_ref[j] - times(inverse_ref[j], back)).astype(BF16))
     place = lax.broadcasted_iota(jnp.int16, (rows, rows), 0) == order_ref[...].astype(jnp.int16)
     pick = jnp.where(place, BF16(1), BF16(0))
-    out_ref[...] = times(pick, jnp.concatenate(solved, axis=0)).astype(BF16)
+    solved = jnp.concatenate(solved, axis=0)
+    half = rows // 2
+    moves = []
+    for k in range(2):
+        part = pl.ds(k * half, half)
+        out_ref[part] = times(pick[k * half : (k + 1) * half], solved).astype(BF16)
+        moves.append(pltpu.make_async_copy(out_ref.at[part], out_hbm.at[part], sems.at[k]))
+        moves[-1].start()
+    for move in moves:
+        move.wait()
 
 
 def on_device(
@@ -244,6 +253,7 @@
         ],
         compiler_params=pltpu.CompilerParams(vmem_limit_bytes=56 * MIB),
     )(order, rhs, leaf_inverse, leaf_column_generator, up, down)
+    term, up = lax.optimization_barrier((term, up))
     pairs = [both(term, 0, col_bits)]
     shared = among_four(share, low, col_bits)
     for level in range(1, low):
@@ -260,9 +270,14 @@
         y, sent = call(functools.partial(down_kernel, level, col_bits), steps, 5, 6 * MIB)(
             both(sent, level, col_bits), pairs[level - 1], y, up, down
         )
-    (solved,) = call(functools.partial(last_kernel, col_bits), [(rhs.shape, BF16)], 8, 24 * MIB)(
-        order, both(sent, 0, col_bits), state, y, up, leaf_inverse, leaf_column_generator, rows
-    )
+    (solved,) = pl.pallas_call(
+        functools.partial(last_kernel, col_bits),
+        out_shape=[jax.ShapeDtypeStruct(rhs.shape, BF16)],
+        in_specs=[pl.BlockSpec(memory_space=pltpu.VMEM)] * 8,
+        out_specs=[pl.BlockSpec(memory_space=pltpu.HBM)],
+        scratch_shapes=[pltpu.VMEM(rhs.shape, BF16), pltpu.SemaphoreType.DMA((2,))],
+        compiler_params=pltpu.CompilerParams(vmem_limit_bytes=24 * MIB),
+    )(order, both(sent, 0, col_bits), state, y, up, leaf_inverse, leaf_column_generator, rows)
     return solved
 
 

time: 135 us -> 135 us (level)
  no operation moved by 1% of the time
where the time goes in v1:
time: 135 us
  blocking collectives  111 us (82%)
  Pallas kernels  11.8 us (9%)
  starting transfers between devices  11 us (8%)
    all_gather x15, blocking collectives, both(): lax.all_gather(value, axis, axis=0, tiled=False, axis_index_groups=groups)  104 us
    all_to_all x1, starting transfers between devices, among_four(): return lax.all_to_all(value, axis, 0, 0, axis_index_groups=groups)  11 us
    all_gather x1, blocking collectives, across_both(): lax.all_gather(value, axis, axis=0, tiled=False, axis_index_groups=groups)  6.69 us
    pallas_call x1, Pallas kernels, on_device(): pl.pallas_call(functools.partial(leaf_kernel, low, col_bits), out_shape=[...  4.71 us
  transfers between devices with their start and end apart: 1, of which 0 were waited for; matrix products, arithmetic and copies ran while one was open for 0% of the time, Pallas kernels for 1%

profile of v1, /device:TPU:1, one launch (start us, length us, event | category | flops | bytes accessed | tf_op | source)
XLA Modules:
  0.0 134.5 jit_solution(9181829195961584314)
XLA Ops:
  0.0 4.7 %shard_map.64 = (f32[2,512,256]{2,1,0:T(8,128)}, f32[256,256]{1,0:T(8,128)}, bf16[256,256]{1,0:T(8,128)(2,1)}, bf16[4,2,256,256]{3,2,1,0:T(8,128)(2,1)}) custom-call(s32[1,1024]{1,0:T(1,128)} %order_ref.1, bf16[1024,256]{1,0:T(8,128)(2,1)} %rhs_hbm.1, bf16[2,512,512]{2,1,0:T(8,128)(2,1)} %inverse_ref.1, bf16[2,512,256]{2,1,0:T(8,128)(2,1)} %basis_ref.1, ...), custom_call_target="tpu_custom_call" | custom-call | tf_op jit(solution)/shard_map/pallas_call | solution.py:231
  4.7 11.0 %all-to-all-start = ((bf16[4,2,256,256]{3,2,1,0:T(8,128)(2,1)}), bf16[4,2,256,256]{3,2,1,0:T(8,128)(2,1)S(1)}, u32[]{:S(2)}, u32[]{:S(2)}) async-start(bf16[4,2,256,256]{3,2,1,0:T(8,128)(2,1)} %get-tuple-element.30), calls=%async_computation | async-start | bytes 2097152 | tf_op jit(solution)/shard_map/all_to_all | solution.py:44
  15.7 2.6 %all-gather = bf16[512,256]{1,0:T(8,128)(2,1)S(1)} all-gather(bf16[256,256]{1,0:T(8,128)(2,1)S(1)} %copy-done.21), channel_id=2, replica_groups={{0,1},{2,3},{4,5},{6,7},{8,9},{10,11},{12,13},{14,15},{16,17},{18,19},{..., dimensions={0}, use_global_device_ids=true | all-gather | bytes 393216 | tf_op jit(solution)/shard_map/all_gather | solution.py:30
  18.5 5.3 %all-gather.1 = bf16[512,256]{1,0:T(8,128)(2,1)S(1)} all-gather(bf16[256,256]{1,0:T(8,128)(2,1)S(1)} %shard_map.65), channel_id=3, replica_groups={{0,2},{1,3},{4,6},{5,7},{8,10},{9,11},{12,14},{13,15},{16,18},{17,19},{..., dimensions={0}, use_global_device_ids=true | all-gather | bytes 393216 | tf_op jit(solution)/shard_map/all_gather | solution.py:30
  24.0 8.8 %all-gather.2 = bf16[512,256]{1,0:T(8,128)(2,1)S(1)} all-gather(bf16[256,256]{1,0:T(8,128)(2,1)S(1)} %shard_map.66), channel_id=4, replica_groups={{0,4},{1,5},{2,6},{3,7},{8,12},{9,13},{10,14},{11,15},{16,20},{17,21},{..., dimensions={0}, use_global_device_ids=true | all-gather | bytes 393216 | tf_op jit(solution)/shard_map/all_gather | solution.py:30
  33.0 10.1 %all-gather.3 = bf16[512,256]{1,0:T(8,128)(2,1)S(1)} all-gather(bf16[256,256]{1,0:T(8,128)(2,1)S(1)} %shard_map.67), channel_id=5, replica_groups={{0,8},{1,9},{2,10},{3,11},{4,12},{5,13},{6,14},{7,15},{16,24},{17,25},{..., dimensions={0}, use_global_device_ids=true | all-gather | bytes 393216 | tf_op jit(solution)/shard_map/all_gather | solution.py:30
  43.3 4.5 %all-gather.4 = bf16[512,256]{1,0:T(8,128)(2,1)S(1)} all-gather(bf16[256,256]{1,0:T(8,128)(2,1)S(1)} %shard_map.68), channel_id=6, replica_groups={{0,16},{32,48},{64,80},{96,112},{128,144},{160,176},{192,208},{224,240}..., dimensions={0}, use_global_device_ids=true | all-gather | bytes 393216 | tf_op jit(solution)/shard_map/all_gather | solution.py:30
  48.0 6.7 %all-gather.5 = bf16[512,256]{1,0:T(8,128)(2,1)S(1)} all-gather(bf16[256,256]{1,0:T(8,128)(2,1)S(1)} %shard_map.69), channel_id=7, replica_groups={{0,32},{16,48},{64,96},{80,112},{128,160},{144,176},{192,224},{208,240}..., dimensions={0}, use_global_device_ids=true | all-gather | bytes 393216 | tf_op jit(solution)/shard_map/all_gather | solution.py:30
  54.9 4.8 %all-gather.6 = bf16[512,256]{1,0:T(8,128)(2,1)S(1)} all-gather(bf16[256,256]{1,0:T(8,128)(2,1)S(1)} %shard_map.70), channel_id=8, replica_groups={{0,64},{16,80},{32,96},{48,112},{128,192},{144,208},{160,224},{176,240}..., dimensions={0}, use_global_device_ids=true | all-gather | bytes 393216 | tf_op jit(solution)/shard_map/all_gather | solution.py:30
  59.9 0.7 copy-done.15
  60.6 7.2 %all-gather.7 = bf16[512,256]{1,0:T(8,128)(2,1)S(1)} all-gather(bf16[256,256]{1,0:T(8,128)(2,1)S(1)} %shard_map.71), channel_id=9, replica_groups={{0,128},{16,144},{32,160},{48,176},{64,192},{80,208},{96,224},{112,240}..., dimensions={0}, use_global_device_ids=true | all-gather | bytes 393216 | tf_op jit(solution)/shard_map/all_gather | solution.py:30
  67.8 6.7 %all-gather.8 = bf16[512,256]{1,0:T(8,128)(2,1)S(1)} all-gather(bf16[256,256]{1,0:T(8,128)(2,1)S(1)} %shard_map.72), channel_id=10, replica_groups={{0,384},{16,400},{32,416},{48,432},{64,448},{80,464},{96,480},{112,496}..., dimensions={0}, use_global_device_ids=true | all-gather | bytes 393216 | tf_op jit(solution)/shard_map/all_gather | solution.py:37
  74.5 0.9 shard_map.73
  75.5 5.8 %all-gather.9 = bf16[512,256]{1,0:T(8,128)(2,1)S(1)} all-gather(bf16[256,256]{1,0:T(8,128)(2,1)S(1)} %get-tuple-element.33), channel_id=11, replica_groups={{0,64},{16,80},{32,96},{48,112},{128,192},{144,208},{160,224},{176,240}..., dimensions={0}, use_global_device_ids=true | all-gather | bytes 393216 | tf_op jit(solution)/shard_map/all_gather | solution.py:30
  81.7 6.0 %all-gather.10 = bf16[512,256]{1,0:T(8,128)(2,1)S(1)} all-gather(bf16[256,256]{1,0:T(8,128)(2,1)S(1)} %get-tuple-element.35), channel_id=12, replica_groups={{0,32},{16,48},{64,96},{80,112},{128,160},{144,176},{192,224},{208,240}..., dimensions={0}, use_global_device_ids=true | all-gather | bytes 393216 | tf_op jit(solution)/shard_map/all_gather | solution.py:30
  87.7 0.4 shard_map.75
  88.1 4.8 %all-gather.11 = bf16[512,256]{1,0:T(8,128)(2,1)S(1)} all-gather(bf16[256,256]{1,0:T(8,128)(2,1)S(1)} %get-tuple-element.37), channel_id=13, replica_groups={{0,16},{32,48},{64,80},{96,112},{128,144},{160,176},{192,208},{224,240}..., dimensions={0}, use_global_device_ids=true | all-gather | bytes 393216 | tf_op jit(solution)/shard_map/all_gather | solution.py:30
  93.4 9.8 %all-gather.12 = bf16[512,256]{1,0:T(8,128)(2,1)S(1)} all-gather(bf16[256,256]{1,0:T(8,128)(2,1)S(1)} %get-tuple-element.39), channel_id=14, replica_groups={{0,8},{1,9},{2,10},{3,11},{4,12},{5,13},{6,14},{7,15},{16,24},{17,25},{..., dimensions={0}, use_global_device_ids=true | all-gather | bytes 393216 | tf_op jit(solution)/shard_map/all_gather | solution.py:30
  103.2 0.4 shard_map.77
  103.6 5.5 %all-gather.13 = bf16[512,256]{1,0:T(8,128)(2,1)S(1)} all-gather(bf16[256,256]{1,0:T(8,128)(2,1)S(1)} %get-tuple-element.41), channel_id=15, replica_groups={{0,4},{1,5},{2,6},{3,7},{8,12},{9,13},{10,14},{11,15},{16,20},{17,21},{..., dimensions={0}, use_global_device_ids=true | all-gather | bytes 393216 | tf_op jit(solution)/shard_map/all_gather | solution.py:30
  109.5 7.5 %all-gather.14 = bf16[512,256]{1,0:T(8,128)(2,1)S(1)} all-gather(bf16[256,256]{1,0:T(8,128)(2,1)S(1)} %get-tuple-element.43), channel_id=16, replica_groups={{0,2},{1,3},{4,6},{5,7},{8,10},{9,11},{12,14},{13,15},{16,18},{17,19},{..., dimensions={0}, use_global_device_ids=true | all-gather | bytes 393216 | tf_op jit(solution)/shard_map/all_gather | solution.py:30
  117.1 0.4 shard_map.79
  117.5 14.8 %all-gather.15 = bf16[512,256]{1,0:T(8,128)(2,1)S(1)} all-gather(bf16[256,256]{1,0:T(8,128)(2,1)S(1)} %get-tuple-element.45), channel_id=17, replica_groups={{0,1},{2,3},{4,5},{6,7},{8,9},{10,11},{12,13},{14,15},{16,17},{18,19},{..., dimensions={0}, use_global_device_ids=true | all-gather | bytes 393216 | tf_op jit(solution)/shard_map/all_gather | solution.py:30
  132.3 2.3 %shard_map.80 = bf16[1024,256]{1,0:T(8,128)(2,1)} custom-call(s32[1,1024]{1,0:T(1,128)S(1)} %copy-done.20, bf16[2,256,256]{2,1,0:T(8,128)(2,1)S(1)} %bitcast.39, f32[256,256]{1,0:T(8,128)S(1)} %copy-done.19, bf16[256,256]{1,0:T(8,128)(2,1)S(1)} %get-tuple-element.47.above_ref, bf16[1,9,256,256]{3,2,1,0:T(8,128)(2,1)S(1)} %copy-done, ...), custom_call_target="tpu_custom_call" | custom-call | tf_op jit(solution)/shard_map/pallas_call | solution.py:273
  (55 shorter events, 2.7 us)
Async XLA Ops:
  4.7 11.0 %copy-start.21 = (bf16[256,256]{1,0:T(8,128)(2,1)S(1)}, bf16[256,256]{1,0:T(8,128)(2,1)}, u32[]{:S(2)}) copy-start(bf16[256,256]{1,0:T(8,128)(2,1)} %get-tuple-element.28) | copy-start | bytes 393220
  4.7 13.6 %copy-start = (bf16[1,9,256,256]{3,2,1,0:T(8,128)(2,1)S(1)}, bf16[1,9,256,256]{3,2,1,0:T(8,128)(2,1)}, u32[]{:S(2)}) copy-start(bf16[1,9,256,256]{3,2,1,0:T(8,128)(2,1)} %up_ref.14) | copy-start | bytes 3538948
  4.7 55.9 %all-to-all-start = ((bf16[4,2,256,256]{3,2,1,0:T(8,128)(2,1)}), bf16[4,2,256,256]{3,2,1,0:T(8,128)(2,1)S(1)}, u32[]{:S(2)}, u32[]{:S(2)}) async-start(bf16[4,2,256,256]{3,2,1,0:T(8,128)(2,1)} %get-tuple-element.30), calls=%async_computation | async-start | bytes 2097152 | tf_op jit(solution)/shard_map/all_to_all | solution.py:44
  18.3 5.7 %copy-start.3 = (bf16[512,256]{1,0:T(8,128)(2,1)}, bf16[512,256]{1,0:T(8,128)(2,1)S(1)}, u32[]{:S(2)}) copy-start(bf16[512,256]{1,0:T(8,128)(2,1)S(1)} %all-gather) | copy-start | bytes 786436
  23.8 9.2 %copy-start.5 = (bf16[512,256]{1,0:T(8,128)(2,1)}, bf16[512,256]{1,0:T(8,128)(2,1)S(1)}, u32[]{:S(2)}) copy-start(bf16[512,256]{1,0:T(8,128)(2,1)S(1)} %all-gather.1) | copy-start | bytes 786436
  32.8 10.5 %copy-start.7 = (bf16[512,256]{1,0:T(8,128)(2,1)}, bf16[512,256]{1,0:T(8,128)(2,1)S(1)}, u32[]{:S(2)}) copy-start(bf16[512,256]{1,0:T(8,128)(2,1)S(1)} %all-gather.2) | copy-start | bytes 786436
  43.1 4.9 %copy-start.9 = (bf16[512,256]{1,0:T(8,128)(2,1)}, bf16[512,256]{1,0:T(8,128)(2,1)S(1)}, u32[]{:S(2)}) copy-start(bf16[512,256]{1,0:T(8,128)(2,1)S(1)} %all-gather.3) | copy-start | bytes 786436
  47.8 7.1 %copy-start.11 = (bf16[512,256]{1,0:T(8,128)(2,1)}, bf16[512,256]{1,0:T(8,128)(2,1)S(1)}, u32[]{:S(2)}) copy-start(bf16[512,256]{1,0:T(8,128)(2,1)S(1)} %all-gather.4) | copy-start | bytes 786436
  54.7 5.0 %copy-start.13 = (bf16[512,256]{1,0:T(8,128)(2,1)}, bf16[512,256]{1,0:T(8,128)(2,1)S(1)}, u32[]{:S(2)}) copy-start(bf16[512,256]{1,0:T(8,128)(2,1)S(1)} %all-gather.5) | copy-start | bytes 786436
  59.7 14.8 %copy-start.1 = (bf16[1,9,256,256]{3,2,1,0:T(8,128)(2,1)S(1)}, bf16[1,9,256,256]{3,2,1,0:T(8,128)(2,1)}, u32[]{:S(2)}) copy-start(bf16[1,9,256,256]{3,2,1,0:T(8,128)(2,1)} %down_ref.13) | copy-start | bytes 3538948
  59.9 0.7 copy-start.15
  60.6 13.9 %copy-start.16 = (bf16[512,256]{1,0:T(8,128)(2,1)S(1)}, bf16[512,256]{1,0:T(8,128)(2,1)}, u32[]{:S(2)}) copy-start(bf16[512,256]{1,0:T(8,128)(2,1)} %copy-done.15) | copy-start | bytes 786436
  74.5 6.7 %copy-start.14 = (bf16[512,256]{1,0:T(8,128)(2,1)S(1)}, bf16[512,256]{1,0:T(8,128)(2,1)}, u32[]{:S(2)}) copy-start(bf16[512,256]{1,0:T(8,128)(2,1)} %copy-done.13) | copy-start | bytes 786436
  81.3 6.4 %copy-start.12 = (bf16[512,256]{1,0:T(8,128)(2,1)S(1)}, bf16[512,256]{1,0:T(8,128)(2,1)}, u32[]{:S(2)}) copy-start(bf16[512,256]{1,0:T(8,128)(2,1)} %copy-done.11) | copy-start | bytes 786436
  87.7 5.3 %copy-start.10 = (bf16[512,256]{1,0:T(8,128)(2,1)S(1)}, bf16[512,256]{1,0:T(8,128)(2,1)}, u32[]{:S(2)}) copy-start(bf16[512,256]{1,0:T(8,128)(2,1)} %copy-done.9) | copy-start | bytes 786436
  93.0 10.2 %copy-start.8 = (bf16[512,256]{1,0:T(8,128)(2,1)S(1)}, bf16[512,256]{1,0:T(8,128)(2,1)}, u32[]{:S(2)}) copy-start(bf16[512,256]{1,0:T(8,128)(2,1)} %copy-done.7) | copy-start | bytes 786436
  103.2 5.9 %copy-start.6 = (bf16[512,256]{1,0:T(8,128)(2,1)S(1)}, bf16[512,256]{1,0:T(8,128)(2,1)}, u32[]{:S(2)}) copy-start(bf16[512,256]{1,0:T(8,128)(2,1)} %copy-done.5) | copy-start | bytes 786436
  109.1 7.9 %copy-start.4 = (bf16[512,256]{1,0:T(8,128)(2,1)S(1)}, bf16[512,256]{1,0:T(8,128)(2,1)}, u32[]{:S(2)}) copy-start(bf16[512,256]{1,0:T(8,128)(2,1)} %copy-done.3) | copy-start | bytes 786436
  117.0 15.2 %copy-start.2 = (bf16[2,512,512]{2,1,0:T(8,128)(2,1)S(1)}, bf16[2,512,512]{2,1,0:T(8,128)(2,1)}, u32[]{:S(2)}) copy-start(bf16[2,512,512]{2,1,0:T(8,128)(2,1)} %inverse_ref.1) | copy-start | bytes 3145732
  117.0 15.2 %copy-start.17 = (bf16[2,512,256]{2,1,0:T(8,128)(2,1)S(1)}, bf16[2,512,256]{2,1,0:T(8,128)(2,1)}, u32[]{:S(2)}) copy-start(bf16[2,512,256]{2,1,0:T(8,128)(2,1)} %basis_ref.1) | copy-start | bytes 1572868
  117.0 15.2 %copy-start.18 = (f32[2,512,256]{2,1,0:T(8,128)S(1)}, f32[2,512,256]{2,1,0:T(8,128)}, u32[]{:S(2)}) copy-start(f32[2,512,256]{2,1,0:T(8,128)} %get-tuple-element.48.rows_ref) | copy-start | bytes 3145732
  117.0 15.2 %copy-start.19 = (f32[256,256]{1,0:T(8,128)S(1)}, f32[256,256]{1,0:T(8,128)}, u32[]{:S(2)}) copy-start(f32[256,256]{1,0:T(8,128)} %get-tuple-element.46.state_ref) | copy-start | bytes 786436
  117.1 15.2 %copy-start.20 = (s32[1,1024]{1,0:T(1,128)S(1)}, s32[1,1024]{1,0:T(1,128)}, u32[]{:S(2)}) copy-start(s32[1,1024]{1,0:T(1,128)} %order_ref.1) | copy-start | bytes 12292

commit v2 on v1

--- a/solution.py
+++ b/solution.py
@@ -203,11 +203,11 @@
     place = lax.broadcasted_iota(jnp.int16, (rows, rows), 0) == order_ref[...].astype(jnp.int16)
     pick = jnp.where(place, BF16(1), BF16(0))
     solved = jnp.concatenate(solved, axis=0)
-    half = rows // 2
+    size = rows // 4
     moves = []
-    for k in range(2):
-        part = pl.ds(k * half, half)
-        out_ref[part] = times(pick[k * half : (k + 1) * half], solved).astype(BF16)
+    for k in range(4):
+        part = pl.ds(k * size, size)
+        out_ref[part] = times(pick[k * size : (k + 1) * size], solved).astype(BF16)
         moves.append(pltpu.make_async_copy(out_ref.at[part], out_hbm.at[part], sems.at[k]))
         moves[-1].start()
     for move in moves:
@@ -275,7 +275,7 @@
         out_shape=[jax.ShapeDtypeStruct(rhs.shape, BF16)],
         in_specs=[pl.BlockSpec(memory_space=pltpu.VMEM)] * 8,
         out_specs=[pl.BlockSpec(memory_space=pltpu.HBM)],
-        scratch_shapes=[pltpu.VMEM(rhs.shape, BF16), pltpu.SemaphoreType.DMA((2,))],
+        scratch_shapes=[pltpu.VMEM(rhs.shape, BF16), pltpu.SemaphoreType.DMA((4,))],
         compiler_params=pltpu.CompilerParams(vmem_limit_bytes=24 * MIB),
     )(order, both(sent, 0, col_bits), state, y, up, leaf_inverse, leaf_column_generator, rows)
     return solved

time: 135 us -> 135 us (level)
  no operation moved by 1% of the time
where the time goes in v2:
time: 135 us; the launch traced here: 134 us
  blocking collectives  111 us (82%)
  Pallas kernels  11.7 us (9%)
  starting transfers between devices  11 us (8%)
    all_gather x15, blocking collectives, both(): lax.all_gather(value, axis, axis=0, tiled=False, axis_index_groups=groups)  104 us
    all_to_all x1, starting transfers between devices, among_four(): return lax.all_to_all(value, axis, 0, 0, axis_index_groups=groups)  11 us
    all_gather x1, blocking collectives, across_both(): lax.all_gather(value, axis, axis=0, tiled=False, axis_index_groups=groups)  6.69 us
    pallas_call x1, Pallas kernels, on_device(): pl.pallas_call(functools.partial(leaf_kernel, low, col_bits), out_shape=[...  4.71 us
  transfers between devices with their start and end apart: 1, of which 0 were waited for; matrix products, arithmetic and copies ran while one was open for 0% of the time, Pallas kernels for 1%

profile of v2, /device:TPU:1, one launch (start us, length us, event | category | flops | bytes accessed | tf_op | source)
XLA Modules:
  0.0 134.5 jit_solution(1393024760001939175)
XLA Ops:
  0.0 4.7 %shard_map.64 = (f32[2,512,256]{2,1,0:T(8,128)}, f32[256,256]{1,0:T(8,128)}, bf16[256,256]{1,0:T(8,128)(2,1)}, bf16[4,2,256,256]{3,2,1,0:T(8,128)(2,1)}) custom-call(s32[1,1024]{1,0:T(1,128)} %order_ref.1, bf16[1024,256]{1,0:T(8,128)(2,1)} %rhs_hbm.1, bf16[2,512,512]{2,1,0:T(8,128)(2,1)} %inverse_ref.1, bf16[2,512,256]{2,1,0:T(8,128)(2,1)} %basis_ref.1, ...), custom_call_target="tpu_custom_call" | custom-call | tf_op jit(solution)/shard_map/pallas_call | solution.py:231
  4.7 11.0 %all-to-all-start = ((bf16[4,2,256,256]{3,2,1,0:T(8,128)(2,1)}), bf16[4,2,256,256]{3,2,1,0:T(8,128)(2,1)S(1)}, u32[]{:S(2)}, u32[]{:S(2)}) async-start(bf16[4,2,256,256]{3,2,1,0:T(8,128)(2,1)} %get-tuple-element.30), calls=%async_computation | async-start | bytes 2097152 | tf_op jit(solution)/shard_map/all_to_all | solution.py:44
  15.7 2.6 %all-gather = bf16[512,256]{1,0:T(8,128)(2,1)S(1)} all-gather(bf16[256,256]{1,0:T(8,128)(2,1)S(1)} %copy-done.21), channel_id=2, replica_groups={{0,1},{2,3},{4,5},{6,7},{8,9},{10,11},{12,13},{14,15},{16,17},{18,19},{..., dimensions={0}, use_global_device_ids=true | all-gather | bytes 393216 | tf_op jit(solution)/shard_map/all_gather | solution.py:30
  18.5 5.3 %all-gather.1 = bf16[512,256]{1,0:T(8,128)(2,1)S(1)} all-gather(bf16[256,256]{1,0:T(8,128)(2,1)S(1)} %shard_map.65), channel_id=3, replica_groups={{0,2},{1,3},{4,6},{5,7},{8,10},{9,11},{12,14},{13,15},{16,18},{17,19},{..., dimensions={0}, use_global_device_ids=true | all-gather | bytes 393216 | tf_op jit(solution)/shard_map/all_gather | solution.py:30
  24.0 8.8 %all-gather.2 = bf16[512,256]{1,0:T(8,128)(2,1)S(1)} all-gather(bf16[256,256]{1,0:T(8,128)(2,1)S(1)} %shard_map.66), channel_id=4, replica_groups={{0,4},{1,5},{2,6},{3,7},{8,12},{9,13},{10,14},{11,15},{16,20},{17,21},{..., dimensions={0}, use_global_device_ids=true | all-gather | bytes 393216 | tf_op jit(solution)/shard_map/all_gather | solution.py:30
  33.0 10.1 %all-gather.3 = bf16[512,256]{1,0:T(8,128)(2,1)S(1)} all-gather(bf16[256,256]{1,0:T(8,128)(2,1)S(1)} %shard_map.67), channel_id=5, replica_groups={{0,8},{1,9},{2,10},{3,11},{4,12},{5,13},{6,14},{7,15},{16,24},{17,25},{..., dimensions={0}, use_global_device_ids=true | all-gather | bytes 393216 | tf_op jit(solution)/shard_map/all_gather | solution.py:30
  43.3 4.5 %all-gather.4 = bf16[512,256]{1,0:T(8,128)(2,1)S(1)} all-gather(bf16[256,256]{1,0:T(8,128)(2,1)S(1)} %shard_map.68), channel_id=6, replica_groups={{0,16},{32,48},{64,80},{96,112},{128,144},{160,176},{192,208},{224,240}..., dimensions={0}, use_global_device_ids=true | all-gather | bytes 393216 | tf_op jit(solution)/shard_map/all_gather | solution.py:30
  48.0 6.7 %all-gather.5 = bf16[512,256]{1,0:T(8,128)(2,1)S(1)} all-gather(bf16[256,256]{1,0:T(8,128)(2,1)S(1)} %shard_map.69), channel_id=7, replica_groups={{0,32},{16,48},{64,96},{80,112},{128,160},{144,176},{192,224},{208,240}..., dimensions={0}, use_global_device_ids=true | all-gather | bytes 393216 | tf_op jit(solution)/shard_map/all_gather | solution.py:30
  54.9 4.8 %all-gather.6 = bf16[512,256]{1,0:T(8,128)(2,1)S(1)} all-gather(bf16[256,256]{1,0:T(8,128)(2,1)S(1)} %shard_map.70), channel_id=8, replica_groups={{0,64},{16,80},{32,96},{48,112},{128,192},{144,208},{160,224},{176,240}..., dimensions={0}, use_global_device_ids=true | all-gather | bytes 393216 | tf_op jit(solution)/shard_map/all_gather | solution.py:30
  59.9 0.7 copy-done.15
  60.6 7.2 %all-gather.7 = bf16[512,256]{1,0:T(8,128)(2,1)S(1)} all-gather(bf16[256,256]{1,0:T(8,128)(2,1)S(1)} %shard_map.71), channel_id=9, replica_groups={{0,128},{16,144},{32,160},{48,176},{64,192},{80,208},{96,224},{112,240}..., dimensions={0}, use_global_device_ids=true | all-gather | bytes 393216 | tf_op jit(solution)/shard_map/all_gather | solution.py:30
  67.8 6.7 %all-gather.8 = bf16[512,256]{1,0:T(8,128)(2,1)S(1)} all-gather(bf16[256,256]{1,0:T(8,128)(2,1)S(1)} %shard_map.72), channel_id=10, replica_groups={{0,384},{16,400},{32,416},{48,432},{64,448},{80,464},{96,480},{112,496}..., dimensions={0}, use_global_device_ids=true | all-gather | bytes 393216 | tf_op jit(solution)/shard_map/all_gather | solution.py:37
  74.5 0.9 shard_map.73
  75.5 5.8 %all-gather.9 = bf16[512,256]{1,0:T(8,128)(2,1)S(1)} all-gather(bf16[256,256]{1,0:T(8,128)(2,1)S(1)} %get-tuple-element.33), channel_id=11, replica_groups={{0,64},{16,80},{32,96},{48,112},{128,192},{144,208},{160,224},{176,240}..., dimensions={0}, use_global_device_ids=true | all-gather | bytes 393216 | tf_op jit(solution)/shard_map/all_gather | solution.py:30
  81.7 6.0 %all-gather.10 = bf16[512,256]{1,0:T(8,128)(2,1)S(1)} all-gather(bf16[256,256]{1,0:T(8,128)(2,1)S(1)} %get-tuple-element.35), channel_id=12, replica_groups={{0,32},{16,48},{64,96},{80,112},{128,160},{144,176},{192,224},{208,240}..., dimensions={0}, use_global_device_ids=true | all-gather | bytes 393216 | tf_op jit(solution)/shard_map/all_gather | solution.py:30
  87.7 0.4 shard_map.75
  88.1 4.8 %all-gather.11 = bf16[512,256]{1,0:T(8,128)(2,1)S(1)} all-gather(bf16[256,256]{1,0:T(8,128)(2,1)S(1)} %get-tuple-element.37), channel_id=13, replica_groups={{0,16},{32,48},{64,80},{96,112},{128,144},{160,176},{192,208},{224,240}..., dimensions={0}, use_global_device_ids=true | all-gather | bytes 393216 | tf_op jit(solution)/shard_map/all_gather | solution.py:30
  93.4 9.8 %all-gather.12 = bf16[512,256]{1,0:T(8,128)(2,1)S(1)} all-gather(bf16[256,256]{1,0:T(8,128)(2,1)S(1)} %get-tuple-element.39), channel_id=14, replica_groups={{0,8},{1,9},{2,10},{3,11},{4,12},{5,13},{6,14},{7,15},{16,24},{17,25},{..., dimensions={0}, use_global_device_ids=true | all-gather | bytes 393216 | tf_op jit(solution)/shard_map/all_gather | solution.py:30
  103.2 0.4 shard_map.77
  103.6 5.5 %all-gather.13 = bf16[512,256]{1,0:T(8,128)(2,1)S(1)} all-gather(bf16[256,256]{1,0:T(8,128)(2,1)S(1)} %get-tuple-element.41), channel_id=15, replica_groups={{0,4},{1,5},{2,6},{3,7},{8,12},{9,13},{10,14},{11,15},{16,20},{17,21},{..., dimensions={0}, use_global_device_ids=true | all-gather | bytes 393216 | tf_op jit(solution)/shard_map/all_gather | solution.py:30
  109.5 7.5 %all-gather.14 = bf16[512,256]{1,0:T(8,128)(2,1)S(1)} all-gather(bf16[256,256]{1,0:T(8,128)(2,1)S(1)} %get-tuple-element.43), channel_id=16, replica_groups={{0,2},{1,3},{4,6},{5,7},{8,10},{9,11},{12,14},{13,15},{16,18},{17,19},{..., dimensions={0}, use_global_device_ids=true | all-gather | bytes 393216 | tf_op jit(solution)/shard_map/all_gather | solution.py:30
  117.1 0.4 shard_map.79
  117.5 14.8 %all-gather.15 = bf16[512,256]{1,0:T(8,128)(2,1)S(1)} all-gather(bf16[256,256]{1,0:T(8,128)(2,1)S(1)} %get-tuple-element.45), channel_id=17, replica_groups={{0,1},{2,3},{4,5},{6,7},{8,9},{10,11},{12,13},{14,15},{16,17},{18,19},{..., dimensions={0}, use_global_device_ids=true | all-gather | bytes 393216 | tf_op jit(solution)/shard_map/all_gather | solution.py:30
  132.3 2.2 %shard_map.80 = bf16[1024,256]{1,0:T(8,128)(2,1)} custom-call(s32[1,1024]{1,0:T(1,128)S(1)} %copy-done.20, bf16[2,256,256]{2,1,0:T(8,128)(2,1)S(1)} %bitcast.39, f32[256,256]{1,0:T(8,128)S(1)} %copy-done.19, bf16[256,256]{1,0:T(8,128)(2,1)S(1)} %get-tuple-element.47.above_ref, bf16[1,9,256,256]{3,2,1,0:T(8,128)(2,1)S(1)} %copy-done, ...), custom_call_target="tpu_custom_call" | custom-call | tf_op jit(solution)/shard_map/pallas_call | solution.py:273
  (55 shorter events, 2.7 us)
Async XLA Ops:
  4.7 11.0 %copy-start.21 = (bf16[256,256]{1,0:T(8,128)(2,1)S(1)}, bf16[256,256]{1,0:T(8,128)(2,1)}, u32[]{:S(2)}) copy-start(bf16[256,256]{1,0:T(8,128)(2,1)} %get-tuple-element.28) | copy-start | bytes 393220
  4.7 13.6 %copy-start = (bf16[1,9,256,256]{3,2,1,0:T(8,128)(2,1)S(1)}, bf16[1,9,256,256]{3,2,1,0:T(8,128)(2,1)}, u32[]{:S(2)}) copy-start(bf16[1,9,256,256]{3,2,1,0:T(8,128)(2,1)} %up_ref.14) | copy-start | bytes 3538948
  4.7 55.9 %all-to-all-start = ((bf16[4,2,256,256]{3,2,1,0:T(8,128)(2,1)}), bf16[4,2,256,256]{3,2,1,0:T(8,128)(2,1)S(1)}, u32[]{:S(2)}, u32[]{:S(2)}) async-start(bf16[4,2,256,256]{3,2,1,0:T(8,128)(2,1)} %get-tuple-element.30), calls=%async_computation | async-start | bytes 2097152 | tf_op jit(solution)/shard_map/all_to_all | solution.py:44
  18.3 5.7 %copy-start.3 = (bf16[512,256]{1,0:T(8,128)(2,1)}, bf16[512,256]{1,0:T(8,128)(2,1)S(1)}, u32[]{:S(2)}) copy-start(bf16[512,256]{1,0:T(8,128)(2,1)S(1)} %all-gather) | copy-start | bytes 786436
  23.8 9.2 %copy-start.5 = (bf16[512,256]{1,0:T(8,128)(2,1)}, bf16[512,256]{1,0:T(8,128)(2,1)S(1)}, u32[]{:S(2)}) copy-start(bf16[512,256]{1,0:T(8,128)(2,1)S(1)} %all-gather.1) | copy-start | bytes 786436
  32.8 10.5 %copy-start.7 = (bf16[512,256]{1,0:T(8,128)(2,1)}, bf16[512,256]{1,0:T(8,128)(2,1)S(1)}, u32[]{:S(2)}) copy-start(bf16[512,256]{1,0:T(8,128)(2,1)S(1)} %all-gather.2) | copy-start | bytes 786436
  43.1 4.9 %copy-start.9 = (bf16[512,256]{1,0:T(8,128)(2,1)}, bf16[512,256]{1,0:T(8,128)(2,1)S(1)}, u32[]{:S(2)}) copy-start(bf16[512,256]{1,0:T(8,128)(2,1)S(1)} %all-gather.3) | copy-start | bytes 786436
  47.8 7.1 %copy-start.11 = (bf16[512,256]{1,0:T(8,128)(2,1)}, bf16[512,256]{1,0:T(8,128)(2,1)S(1)}, u32[]{:S(2)}) copy-start(bf16[512,256]{1,0:T(8,128)(2,1)S(1)} %all-gather.4) | copy-start | bytes 786436
  54.7 5.0 %copy-start.13 = (bf16[512,256]{1,0:T(8,128)(2,1)}, bf16[512,256]{1,0:T(8,128)(2,1)S(1)}, u32[]{:S(2)}) copy-start(bf16[512,256]{1,0:T(8,128)(2,1)S(1)} %all-gather.5) | copy-start | bytes 786436
  59.7 14.8 %copy-start.1 = (bf16[1,9,256,256]{3,2,1,0:T(8,128)(2,1)S(1)}, bf16[1,9,256,256]{3,2,1,0:T(8,128)(2,1)}, u32[]{:S(2)}) copy-start(bf16[1,9,256,256]{3,2,1,0:T(8,128)(2,1)} %down_ref.13) | copy-start | bytes 3538948
  59.9 0.7 copy-start.15
  60.6 13.9 %copy-start.16 = (bf16[512,256]{1,0:T(8,128)(2,1)S(1)}, bf16[512,256]{1,0:T(8,128)(2,1)}, u32[]{:S(2)}) copy-start(bf16[512,256]{1,0:T(8,128)(2,1)} %copy-done.15) | copy-start | bytes 786436
  74.5 6.7 %copy-start.14 = (bf16[512,256]{1,0:T(8,128)(2,1)S(1)}, bf16[512,256]{1,0:T(8,128)(2,1)}, u32[]{:S(2)}) copy-start(bf16[512,256]{1,0:T(8,128)(2,1)} %copy-done.13) | copy-start | bytes 786436
  81.3 6.4 %copy-start.12 = (bf16[512,256]{1,0:T(8,128)(2,1)S(1)}, bf16[512,256]{1,0:T(8,128)(2,1)}, u32[]{:S(2)}) copy-start(bf16[512,256]{1,0:T(8,128)(2,1)} %copy-done.11) | copy-start | bytes 786436
  87.7 5.3 %copy-start.10 = (bf16[512,256]{1,0:T(8,128)(2,1)S(1)}, bf16[512,256]{1,0:T(8,128)(2,1)}, u32[]{:S(2)}) copy-start(bf16[512,256]{1,0:T(8,128)(2,1)} %copy-done.9) | copy-start | bytes 786436
  93.0 10.2 %copy-start.8 = (bf16[512,256]{1,0:T(8,128)(2,1)S(1)}, bf16[512,256]{1,0:T(8,128)(2,1)}, u32[]{:S(2)}) copy-start(bf16[512,256]{1,0:T(8,128)(2,1)} %copy-done.7) | copy-start | bytes 786436
  103.2 5.9 %copy-start.6 = (bf16[512,256]{1,0:T(8,128)(2,1)S(1)}, bf16[512,256]{1,0:T(8,128)(2,1)}, u32[]{:S(2)}) copy-start(bf16[512,256]{1,0:T(8,128)(2,1)} %copy-done.5) | copy-start | bytes 786436
  109.1 7.9 %copy-start.4 = (bf16[512,256]{1,0:T(8,128)(2,1)S(1)}, bf16[512,256]{1,0:T(8,128)(2,1)}, u32[]{:S(2)}) copy-start(bf16[512,256]{1,0:T(8,128)(2,1)} %copy-done.3) | copy-start | bytes 786436
  117.0 15.2 %copy-start.2 = (bf16[2,512,512]{2,1,0:T(8,128)(2,1)S(1)}, bf16[2,512,512]{2,1,0:T(8,128)(2,1)}, u32[]{:S(2)}) copy-start(bf16[2,512,512]{2,1,0:T(8,128)(2,1)} %inverse_ref.1) | copy-start | bytes 3145732
  117.0 15.2 %copy-start.17 = (bf16[2,512,256]{2,1,0:T(8,128)(2,1)S(1)}, bf16[2,512,256]{2,1,0:T(8,128)(2,1)}, u32[]{:S(2)}) copy-start(bf16[2,512,256]{2,1,0:T(8,128)(2,1)} %basis_ref.1) | copy-start | bytes 1572868
  117.0 15.2 %copy-start.18 = (f32[2,512,256]{2,1,0:T(8,128)S(1)}, f32[2,512,256]{2,1,0:T(8,128)}, u32[]{:S(2)}) copy-start(f32[2,512,256]{2,1,0:T(8,128)} %get-tuple-element.48.rows_ref) | copy-start | bytes 3145732
  117.0 15.2 %copy-start.19 = (f32[256,256]{1,0:T(8,128)S(1)}, f32[256,256]{1,0:T(8,128)}, u32[]{:S(2)}) copy-start(f32[256,256]{1,0:T(8,128)} %get-tuple-element.46.state_ref) | copy-start | bytes 786436
  117.1 15.2 %copy-start.20 = (s32[1,1024]{1,0:T(1,128)S(1)}, s32[1,1024]{1,0:T(1,128)}, u32[]{:S(2)}) copy-start(s32[1,1024]{1,0:T(1,128)} %order_ref.1) | copy-start | bytes 12292
